TPU v7x, 128 devices: a whole 4x4x4 slice. The times are simulated.
128 devices in a mesh: subset: 8 (over y, z_lo), tile: 16 (over z_hi, x, core).
Axes of the slice: x: 4, y: 4, z: 4 (z_hi: 2, z_lo: 2; z = z_hi * 2 + z_lo), core: 2. Of those that a mesh axis runs over, the one named last changes fastest.
Arguments:
- start_volume: bfloat16 [8, 64, 65536], P(None, None, 'tile'), may hold values from 0 to 2
- measured: bfloat16 [8, 8, 64, 2048], P('subset'), may hold values from 6528 to 26112
- system_values: bfloat16 [8, 2048, 65536], P('subset', None, 'tile'), may hold values from 0.05 to 2088.96, as said below
- block_pattern: int32 [8, 16, 512], P('subset', None, 'tile'), may hold values from 0 to 1, as said below
- subset_order: int32 [64, 8], replicated, may hold values from 0 to 7, each once within a row
Outputs:
- volume_out: bfloat16 [8, 64, 65536], P(None, None, 'tile')
Inputs may be any that keep to these rules, and one draw needn't show every extreme that they name: `block_pattern`: each entry is 0 or 1; every block row and every block column of each subset's matrix within every 4096-voxel tile holds at least one 1. `system_values`: positive entries. `subset_order`: each row is a permutation of the 8 subsets.
All inputs are finite; a program needn't handle non-finite values.
Results may differ from a plain program's by a relative error of at most 0.0034.
Values may be sent and summed in bfloat16 or wider, within the bound.
A program may use at most 128 MiB of HBM per device.

v0:
```python
import jax
import jax.numpy as jnp
from jax import lax
from jax.sharding import PartitionSpec as P

BLOCK_SIDE = 128
SWEEP_PASSES = 4


def passed_along(block, axis, distance):
    devices = range(lax.axis_size(axis))
    route = [((i - distance) % len(devices), i) for i in devices]
    return lax.ppermute(block, axis, route)


def body(start_volume, measured, system_values, block_pattern, subset_order):
    owner_idx = lax.axis_index("subset")
    holder_count = lax.axis_size("subset")
    pattern = block_pattern[0].astype(jnp.bfloat16)
    matrix = system_values[0] * jnp.repeat(jnp.repeat(pattern, BLOCK_SIDE, 0), BLOCK_SIDE, 1)
    column_sum = jnp.sum(matrix, axis=0, dtype=jnp.float32)
    row_part = jnp.sum(matrix, axis=1, dtype=jnp.float32)[None, :]
    slice_measurement = measured[0]

    def subset_selector(slice_portion):
        source = (owner_idx - slice_portion) % holder_count
        return (subset_order == source).astype(jnp.bfloat16)

    volume = jnp.einsum(
        "sf,fsv->sv", subset_selector(0), start_volume, preferred_element_type=jnp.float32
    )
    ray_total = lax.psum(row_part, "tile")
    for slice_portion in range(SWEEP_PASSES):
        selected_subset = subset_selector(slice_portion)
        destination_rows = jnp.einsum(
            "ej,jev->ev", selected_subset, slice_measurement, preferred_element_type=jnp.float32
        )
        narrow = volume.astype(jnp.bfloat16)
        partial_value = lax.dot_general(
            narrow, matrix, (((1,), (1,)), ((), ())), preferred_element_type=jnp.float32
        )
        projected = lax.psum(partial_value, "tile")
        residue = ((destination_rows - projected) / ray_total).astype(jnp.bfloat16)
        spread_back = jnp.dot(residue, matrix, preferred_element_type=jnp.float32)
        volume = volume + spread_back / column_sum[None, :]
        if slice_portion + 1 < SWEEP_PASSES:
            volume = passed_along(volume, "subset", 1)
    final_pick = subset_selector(SWEEP_PASSES - 1).astype(jnp.float32)
    rounded = lax.optimization_barrier(volume.astype(jnp.bfloat16)).astype(jnp.float32)
    contribution = jnp.transpose(final_pick)[:, :, None] * rounded[None, :, :]
    gathered = lax.psum(contribution.astype(jnp.bfloat16), "subset")
    return gathered


def solution(mesh):
    placed = (
        P(None, None, "tile"),
        P("subset", None, None, None),
        P("subset", None, "tile"),
        P("subset", None, "tile"),
        P(),
    )
    return jax.shard_map(
        body, mesh=mesh, in_specs=placed, out_specs=P(None, None, "tile"), check_vma=False
    )
```

profile of v0, /device:TPU:1, one launch (start us, length us, event | category | flops | bytes accessed | tf_op | source)
XLA Modules:
  0.0 965.1 jit_solution(6587851373304264414)
XLA Ops:
  8.3 25.4 %broadcast_in_dim.7 = bf16[2048,32,128]{2,1,0:T(8,128)(2,1)S(1)} broadcast(bf16[2048,32]{1,0:T(8,128)(2,1)S(1)} %bitcast.70), dimensions={0,1} | broadcast | bytes 16908288 | tf_op jit(solution)/shard_map/broadcast_in_dim | solution.py:20
  33.7 14.5 %convert_reduce_fusion.1 = (f32[2048]{0:T(1024)S(1)}, f32[4096]{0:T(1024)S(1)}, bf16[2048,4096]{1,0:T(8,128)(2,1)}) fusion(bf16[256,8,32,128]{3,2,1,0:T(8,128)(2,1)S(1)} %bitcast.69, bf16[1,2048,4096]{2,1,0:T(8,128)(2,1)} %param.7), kind=kLoop, calls=%fused_computation.1 | loop fusion | flops 33548288 | bytes 50356224 | tf_op jit(solution)/shard_map/reduce_sum | solution.py:22
  48.2 5.0 fusion.5
  53.2 11.8 %fusion.15 = f32[64,2048]{1,0:T(8,128)} fusion(bf16[2048,4096]{1,0:T(8,128)(2,1)} %get-tuple-element.9, f32[64,1,4096]{2,1,0:T(1,128)S(1)} %fusion.5), kind=kOutput, calls=%fused_computation.24 | convolution fusion | flops 1073741824 | bytes 18350080 | tf_op jit(solution)/shard_map/dot_general | solution.py:39
  65.6 35.4 %psum.43 = f32[2048]{0:T(1024)S(1)} all-reduce(f32[2048]{0:T(1024)S(1)} %get-tuple-element.5), channel_id=1, replica_groups=mesh['subset'=8,'tile'=16] {'tile'}, use_global_device_ids=true, to_apply=%region_2.3 | all-reduce | flops 2048 | bytes 16384 | tf_op jit(solution)/shard_map/psum | solution.py:32
  103.4 104.8 %all-reduce.6.cloned.1.call-done = f32[64,2048]{1,0:T(8,128)} async-done(((f32[64,2048]{1,0:T(8,128)}), f32[64,2048]{1,0:T(8,128)}) %all-reduce.6.cloned.1.call-update) | async-done | bytes 524304 | tf_op jit(solution)/shard_map/psum | solution.py:42
  208.1 9.6 fusion.3
  218.2 25.8 %collective-permute-done = f32[64,4096]{1,0:T(8,128)S(1)} collective-permute-done((f32[64,4096]{1,0:T(8,128)S(1)}, f32[64,4096]{1,0:T(8,128)S(1)}, u32[]{:S(2)}, u32[]{:S(2)}) %collective-permute-start) | collective-permute-done | bytes 1048608 | tf_op jit(solution)/shard_map/ppermute | solution.py:13
  244.0 11.7 %fusion.28 = f32[64,2048]{1,0:T(8,128)} fusion(bf16[2048,4096]{1,0:T(8,128)(2,1)} %get-tuple-element.9, f32[64,4096]{1,0:T(8,128)S(1)} %collective-permute-done), kind=kOutput, calls=%fused_computation.41 | convolution fusion | flops 1074003968 | bytes 18350080 | tf_op jit(solution)/shard_map/dot_general | solution.py:39
  256.1 2.4 fusion.11
  258.4 133.3 %all-reduce.8.cloned.1.call-done = f32[64,2048]{1,0:T(8,128)} async-done(((f32[64,2048]{1,0:T(8,128)}), f32[64,2048]{1,0:T(8,128)}) %all-reduce.8.cloned.1.call-update) | async-done | bytes 524304 | tf_op jit(solution)/shard_map/psum | solution.py:42
  391.8 9.2 fusion.2
  401.4 25.8 %collective-permute-done.1 = f32[64,4096]{1,0:T(8,128)S(1)} collective-permute-done((f32[64,4096]{1,0:T(8,128)S(1)}, f32[64,4096]{1,0:T(8,128)S(1)}, u32[]{:S(2)}, u32[]{:S(2)}) %collective-permute-start.1) | collective-permute-done | bytes 1048608 | tf_op jit(solution)/shard_map/ppermute | solution.py:13
  427.1 11.7 %fusion.26 = f32[64,2048]{1,0:T(8,128)} fusion(bf16[2048,4096]{1,0:T(8,128)(2,1)} %get-tuple-element.9, f32[64,4096]{1,0:T(8,128)S(1)} %collective-permute-done.1), kind=kOutput, calls=%fused_computation.39 | convolution fusion | flops 1074003968 | bytes 18350080 | tf_op jit(solution)/shard_map/dot_general | solution.py:39
  439.1 2.4 fusion.9
  441.4 133.5 %all-reduce.10.cloned.1.call-done = f32[64,2048]{1,0:T(8,128)} async-done(((f32[64,2048]{1,0:T(8,128)}), f32[64,2048]{1,0:T(8,128)}) %all-reduce.10.cloned.1.call-update) | async-done | bytes 524304 | tf_op jit(solution)/shard_map/psum | solution.py:42
  574.9 9.2 fusion.1
  584.7 25.8 %collective-permute-done.2 = f32[64,4096]{1,0:T(8,128)S(1)} collective-permute-done((f32[64,4096]{1,0:T(8,128)S(1)}, f32[64,4096]{1,0:T(8,128)S(1)}, u32[]{:S(2)}, u32[]{:S(2)}) %collective-permute-start.2) | collective-permute-done | bytes 1048608 | tf_op jit(solution)/shard_map/ppermute | solution.py:13
  610.5 11.7 %fusion.24 = f32[64,2048]{1,0:T(8,128)} fusion(bf16[2048,4096]{1,0:T(8,128)(2,1)} %get-tuple-element.9, f32[64,4096]{1,0:T(8,128)S(1)} %collective-permute-done.2), kind=kOutput, calls=%fused_computation.37 | convolution fusion | flops 1074003968 | bytes 18350080 | tf_op jit(solution)/shard_map/dot_general | solution.py:39
  624.8 133.5 %all-reduce.12.cloned.1.call-done = f32[64,2048]{1,0:T(8,128)} async-done(((f32[64,2048]{1,0:T(8,128)}), f32[64,2048]{1,0:T(8,128)}) %all-reduce.12.cloned.1.call-update) | async-done | bytes 524304 | tf_op jit(solution)/shard_map/psum | solution.py:42
  758.3 9.2 fusion.4
  767.6 3.1 multiply_convert_fusion
  770.7 182.9 %all-reduce.14.cloned.1.call-done = bf16[8,64,4096]{2,1,0:T(8,128)(2,1)} async-done(((bf16[8,64,4096]{2,1,0:T(8,128)(2,1)}), bf16[8,64,4096]{2,1,0:T(8,128)(2,1)}) %all-reduce.14.cloned.1.call-update) | async-done | bytes 4194320 | tf_op jit(solution)/shard_map/psum | solution.py:51
  953.6 4.7 copy.46
  (27 shorter events, 9.3 us)
Async XLA Ops:
  6.5 94.5 %copy-start = (bf16[1,8,64,2048]{3,2,1,0:T(8,128)(2,1)S(1)}, bf16[1,8,64,2048]{3,2,1,0:T(8,128)(2,1)}, u32[]{:S(2)}) copy-start(bf16[1,8,64,2048]{3,2,1,0:T(8,128)(2,1)} %param.6) | copy-start | bytes 6291460
  6.5 201.6 %all-reduce.6.cloned.1.call-start = ((), (), s32[]{:S(2)}) async-start(), calls=%async_computation | async-start | bytes 1048576 | tf_op jit(solution)/shard_map/psum | solution.py:42
  33.7 14.5 %copy-start.1 = (bf16[8,64,4096]{2,1,0:T(8,128)(2,1)S(1)}, bf16[8,64,4096]{2,1,0:T(8,128)(2,1)}, u32[]{:S(2)}) copy-start(bf16[8,64,4096]{2,1,0:T(8,128)(2,1)} %param.5) | copy-start | bytes 12582916
  65.1 326.7 %all-reduce.8.cloned.1.call-start = ((), (), s32[]{:S(2)}) async-start(), calls=%async_computation.1 | async-start | bytes 1048576 | tf_op jit(solution)/shard_map/psum | solution.py:42
  217.7 26.2 %collective-permute-start = (f32[64,4096]{1,0:T(8,128)S(1)}, f32[64,4096]{1,0:T(8,128)S(1)}, u32[]{:S(2)}, u32[]{:S(2)}) collective-permute-start(f32[64,4096]{1,0:T(8,128)S(1)} %fusion.3), channel_id=1, source_target_pairs={{112,0},{0,16},{16,32},{32,48},{48,64},{64,80},{80,96},{96,112},{1... | collective-permute-start | bytes 3145736 | tf_op jit(solution)/shard_map/ppermute | solution.py:13
  255.7 319.2 %all-reduce.10.cloned.1.call-start = ((), (), s32[]{:S(2)}) async-start(), calls=%async_computation.2 | async-start | bytes 1048576 | tf_op jit(solution)/shard_map/psum | solution.py:42
  400.9 26.2 %collective-permute-start.1 = (f32[64,4096]{1,0:T(8,128)S(1)}, f32[64,4096]{1,0:T(8,128)S(1)}, u32[]{:S(2)}, u32[]{:S(2)}) collective-permute-start(f32[64,4096]{1,0:T(8,128)S(1)} %fusion.2), channel_id=1, source_target_pairs={{112,0},{0,16},{16,32},{32,48},{48,64},{64,80},{80,96},{96,112},{1... | collective-permute-start | bytes 3145736 | tf_op jit(solution)/shard_map/ppermute | solution.py:13
  438.9 319.4 %all-reduce.12.cloned.1.call-start = ((), (), s32[]{:S(2)}) async-start(), calls=%async_computation.3 | async-start | bytes 1048576 | tf_op jit(solution)/shard_map/psum | solution.py:42
  584.1 26.4 %collective-permute-start.2 = (f32[64,4096]{1,0:T(8,128)S(1)}, f32[64,4096]{1,0:T(8,128)S(1)}, u32[]{:S(2)}, u32[]{:S(2)}) collective-permute-start(f32[64,4096]{1,0:T(8,128)S(1)} %fusion.1), channel_id=1, source_target_pairs={{112,0},{0,16},{16,32},{32,48},{48,64},{64,80},{80,96},{96,112},{1... | collective-permute-start | bytes 3145736 | tf_op jit(solution)/shard_map/ppermute | solution.py:13
  622.3 331.4 %all-reduce.14.cloned.1.call-start = ((), (), s32[]{:S(2)}) async-start(), calls=%async_computation.4 | async-start | bytes 8388608 | tf_op jit(solution)/shard_map/psum | solution.py:51
Sparse Core Ops, SparseCore 0:
  65.2 142.8 all-reduce.5
  255.9 135.8 all-reduce.7
  439.0 135.8 all-reduce.9
  622.4 135.8 all-reduce.11
  770.8 182.7 all-reduce.13
where the time goes:
time: 975 us; the launch traced here: 965 us
  waiting for transfers between devices  765 us (78%)
  matrix products  98.5 us (10%)
  blocking collectives  35.4 us (4%)
  local copies, waits for them, and re-layouts  30.7 us (3%)
  other arithmetic  19.2 us (2%)
  between operations  13.4 us (1%)
    psum x4, waiting for transfers between devices, body(): projected = lax.psum(partial_value, 'tile')  505 us
    psum x1, waiting for transfers between devices, body(): gathered = lax.psum(contribution.astype(jnp.bfloat16), 'subset')  183 us
    ppermute x3, waiting for transfers between devices, passed_along(): return lax.ppermute(block, axis, route)  77.3 us
    dot_general x4, matrix products, body(): lax.dot_general(narrow, matrix, (((1,), (1,)), ((), ())), preferred_eleme...  47.1 us
    dot_general x4, matrix products, body(): spread_back = jnp.dot(residue, matrix, preferred_element_type=jnp.float32)  37.1 us
    psum x1, blocking collectives, body(): ray_total = lax.psum(row_part, 'tile')  35.4 us
    broadcast_in_dim x1, local copies, waits for them, and re-layouts, body(): jnp.repeat(jnp.repeat(pattern, BLOCK_SIDE, 0), BLOCK_SIDE, 1)  25.4 us
  transfers between devices with their start and end apart: 8, of which 8 were waited for; matrix products, arithmetic and copies ran while one was open for 1% of the time, Pallas kernels for 0%

commit v1 on v0

v1 whole, which is shorter than its diff:
```python
import functools

import jax
import jax.numpy as jnp
from jax import lax
from jax.experimental import pallas as pl
from jax.experimental.pallas import tpu as pltpu
from jax.sharding import PartitionSpec as P

MESH = pl.DeviceIdType.MESH
F32 = jnp.float32
BF16 = jnp.bfloat16
SIDE = 128
PASSES = 4
ONES = 16
NT = (((1,), (1,)), ((), ()))
NN = (((1,), (0,)), ((), ()))


def dot(a, b, dims):
    return lax.dot_general(a, b, dims, preferred_element_type=F32)


def sweep_kernel(
    tiles, order_ref, mask_ref, start_hbm, meas_hbm, sys_hbm, out_hbm,
    a_ref, start_ref, vb_ref, meas_ref, dest_ref, rows_ref, inv_ref, part, recv, resid,
    hi_out, lo_out, hi_in, lo_in, acc, gat,
    a_sem, io_sem, rs_send, rs_recv, ag_send, ag_recv, hop_send, hop_recv, fin_send, fin_recv, out_sem,
):
    me_s, me_t = lax.axis_index("subset"), lax.axis_index("tile")
    subsets = order_ref.shape[1]
    slices = order_ref.shape[0]
    rays, vox = a_ref.shape
    chunk = rays // tiles
    pair = 2 * chunk
    pairs = rays // pair
    chunks = hop_send.shape[2]
    width = vox // chunks

    def tile_at(d):
        return lax.rem(me_t + d, tiles)

    def subset_at(d):
        return lax.rem(me_s + d, subsets)

    def remote(src, dst, send, recv_, s, t):
        return pltpu.make_async_remote_copy(
            src_ref=src, dst_ref=dst, send_sem=send, recv_sem=recv_,
            device_id=(s, t), device_id_type=MESH,
        )

    def cols(n):
        return pl.ds(pl.multiple_of(n * width, width), width)

    def rays_of(c):
        return pl.ds(pl.multiple_of(c * chunk, chunk), chunk)

    start_copy = pltpu.make_async_copy(start_hbm, start_ref, io_sem.at[0])
    start_copy.start()
    half = lax.div(me_t, 2)

    def block_rows(i):
        return pl.ds(pl.multiple_of(lax.rem(half + i, pairs) * pair, pair), pair)

    def matrix_copy(i):
        return pltpu.make_async_copy(
            sys_hbm.at[0, block_rows(i), :], a_ref.at[block_rows(i), :], a_sem.at[i]
        )

    for i in range(pairs):
        matrix_copy(i).start()
    meas_copy = pltpu.make_async_copy(
        meas_hbm.at[0, :, :, rays_of(me_t)], meas_ref, io_sem.at[1]
    )
    meas_copy.start()

    barrier = pltpu.get_barrier_semaphore()
    for d in range(1, tiles):
        pl.semaphore_signal(barrier, inc=1, device_id=(me_s, tile_at(d)), device_id_type=MESH)
    for d in range(1, subsets):
        pl.semaphore_signal(barrier, inc=1, device_id=(subset_at(d), me_t), device_id_type=MESH)

    vb_ref[slices:, :] = jnp.ones((ONES, vox), BF16)
    resid[0, slices:, :] = jnp.ones((ONES, rays), BF16)

    start_copy.wait()

    @pl.loop(0, chunks)
    def _(n):
        total = jnp.zeros((slices, width), F32)
        for f in range(subsets):
            weight = (order_ref[:, f : f + 1] == me_s).astype(F32)
            total += weight * start_ref[f, :, cols(n)].astype(F32)
        vb_ref[:slices, cols(n)] = total.astype(BF16)

    pl.semaphore_wait(barrier, tiles - 1 + subsets - 1)

    def rs_copy(j, d, c, height):
        return remote(
            part.at[c, pl.ds(0, height), :], recv.at[j, d, pl.ds(0, height), :],
            rs_send.at[d], rs_recv.at[j, d], me_s, tile_at(d),
        )

    @pl.loop(0, pairs)
    def _(i):
        matrix_copy(i).wait()
        b = lax.rem(half + i, pairs)
        per_pair = pair // SIDE
        for q in range(per_pair):
            mask = jnp.broadcast_to(mask_ref[pl.ds(b * per_pair + q, 1), :], (16, vox)).astype(BF16)
            for u in range(SIDE // 16):
                here = pl.ds(pl.multiple_of(b * pair + q * SIDE + u * 16, 16), 16)
                a_ref[here, :] = a_ref[here, :] * mask
        p = dot(vb_ref[...], a_ref[block_rows(i), :], NT)
        sums = p[slices:, :]
        high = sums.astype(BF16)
        rest = sums - high.astype(F32)
        mid = rest.astype(BF16)
        low = (rest - mid.astype(F32)).astype(BF16)
        row = lax.broadcasted_iota(jnp.int32, sums.shape, 0)
        packed = jnp.where(
            row == 0, high.astype(F32),
            jnp.where(row == 1, mid.astype(F32), jnp.where(row == 2, low.astype(F32), 0.0)),
        ).astype(BF16)
        for h in range(2):
            c = 2 * b + h
            part[c, pl.ds(0, slices), :] = p[:slices, h * chunk : (h + 1) * chunk].astype(BF16)
            part[c, pl.ds(slices, ONES), :] = packed[:, h * chunk : (h + 1) * chunk]
            d = lax.rem(c + tiles - me_t, tiles)

            @pl.when(d != 0)
            def _():
                rs_copy(0, d, c, slices + ONES).start()

    meas_copy.wait()
    for j in range(PASSES):
        source = lax.rem(me_s + subsets - j, subsets)
        total = jnp.zeros((slices, chunk), F32)
        for f in range(subsets):
            weight = (order_ref[:, f : f + 1] == source).astype(F32)
            total += weight * meas_ref[f].astype(F32)
        dest_ref[j] = total

    def ag_copy(j, d):
        here = resid.at[j, pl.ds(0, slices), rays_of(me_t)]
        return remote(here, here, ag_send.at[d], ag_recv.at[j, d], me_s, tile_at(d))

    def ag_arrival(j, d):
        here = resid.at[j, pl.ds(0, slices), rays_of(lax.rem(me_t + tiles - d, tiles))]
        return remote(here, here, ag_send.at[d], ag_recv.at[j, d], me_s, tile_at(d))

    def hi_copy(j, n):
        return remote(
            hi_out.at[j, :, cols(n)], hi_in.at[j, :, cols(n)],
            hop_send.at[j, 0, n], hop_recv.at[j, 0, n], subset_at(1), me_t,
        )

    def lo_copy(j, n):
        return remote(
            lo_out.at[j, :, cols(n)], lo_in.at[j, :, cols(n)],
            hop_send.at[j, 1, n], hop_recv.at[j, 1, n], subset_at(1), me_t,
        )

    zp = me_s + 1 - 2 * lax.rem(me_s, 2)
    yp, ym, y2 = subset_at(2), subset_at(subsets - 2), subset_at(subsets // 2)
    zp_p = lax.rem(zp + 2, subsets)
    zp_m = lax.rem(zp + subsets - 2, subsets)
    zp_2 = lax.rem(zp + subsets // 2, subsets)

    def fin_copy(kind, block, n, target):
        here = gat.at[block, :, cols(n)]
        return remote(here, here, fin_send.at[kind, n], fin_recv.at[kind, n], target, me_t)

    for j in range(PASSES):
        height = slices + ONES if j == 0 else slices
        if j > 0:
            acc[...] = jnp.zeros_like(acc)

            @pl.loop(0, chunks)
            def _(n):
                hi_copy(j - 1, n).wait_recv()
                acc[...] += dot(hi_in[j - 1, :, cols(n)], a_ref[:, cols(n)], NT)

            for c in range(tiles):
                part[c, pl.ds(0, slices), :] = acc[:, c * chunk : (c + 1) * chunk].astype(BF16)
            for d in range(1, tiles):
                rs_copy(j, d, tile_at(d), slices).start()

            @pl.loop(0, chunks // 2)
            def _(n):
                lo_copy(j - 1, n).start()

        total = part[me_t].astype(F32) if j == 0 else part[me_t, pl.ds(0, slices), :].astype(F32)
        for d in range(1, tiles):
            rs_copy(j, d, tile_at(d), height).wait_recv()
            total += recv[j, d, pl.ds(0, height), :].astype(F32)
        if j == 0:
            rows_ref[...] = jnp.sum(total[slices:, :], axis=0, keepdims=True)
        value = (dest_ref[j] - total[:slices, :]) / rows_ref[...]
        resid[j, pl.ds(0, slices), rays_of(me_t)] = value.astype(BF16)
        for d in range(1, tiles):
            ag_copy(j, d).start()
        if j > 0:
            @pl.loop(chunks // 2, chunks)
            def _(n):
                lo_copy(j - 1, n).start()
        for d in range(1, tiles):
            rs_copy(j, d, tile_at(d), height).wait_send()
        for d in range(1, tiles):
            ag_arrival(j, d).wait_recv()

        @pl.loop(0, chunks)
        def _(n):
            here = cols(n)
            if j == 0:
                back = dot(resid[0], a_ref[:, here], NN)
                inv = 1.0 / back[slices : slices + 1, :]
                inv_ref[:, here] = inv
                base = vb_ref[:slices, here].astype(F32)
            else:
                back = dot(resid[j, pl.ds(0, slices), :], a_ref[:, here], NN)
                inv = inv_ref[:, here]
                lo_copy(j - 1, n).wait_recv()
                base = hi_in[j - 1, :, here].astype(F32) + lo_in[j - 1, :, here].astype(F32)
            volume = base + back[:slices, :] * inv
            high = volume.astype(BF16)
            if j + 1 < PASSES:
                hi_out[j, :, here] = high
                lo_out[j, :, here] = (volume - high.astype(F32)).astype(BF16)
                hi_copy(j, n).start()
            else:
                gat[me_s, :, here] = high
                fin_copy(0, me_s, n, zp).start()
                fin_copy(1, me_s, n, yp).start()
                fin_copy(2, me_s, n, ym).start()

        for d in range(1, tiles):
            ag_copy(j, d).wait_send()

    @pl.loop(0, chunks)
    def _(n):
        fin_copy(1, ym, n, me_s).wait_recv()
        fin_copy(2, yp, n, me_s).wait_recv()

        @pl.when(lax.rem(n, 2) == 0)
        def _():
            fin_copy(3, ym, n, yp).start()

        @pl.when(lax.rem(n, 2) == 1)
        def _():
            fin_copy(3, yp, n, ym).start()

    @pl.loop(0, chunks)
    def _(n):
        fin_copy(0, zp, n, me_s).wait_recv()
        fin_copy(4, zp, n, yp).start()
        fin_copy(5, zp, n, ym).start()

    def out_copy(block, i):
        return pltpu.make_async_copy(gat.at[block], out_hbm.at[block], out_sem.at[i])

    for i, block in enumerate((me_s, zp, yp, ym)):
        out_copy(block, i).start()

    @pl.loop(0, chunks)
    def _(n):
        fin_copy(3, y2, n, me_s).wait_recv()
        fin_copy(6, y2, n, zp).start()

    out_copy(y2, 4).start()

    @pl.loop(0, chunks)
    def _(n):
        fin_copy(4, zp_m, n, me_s).wait_recv()
        fin_copy(5, zp_p, n, me_s).wait_recv()

    out_copy(zp_m, 5).start()
    out_copy(zp_p, 6).start()

    @pl.loop(0, chunks)
    def _(n):
        fin_copy(6, zp_2, n, me_s).wait_recv()

    out_copy(zp_2, 7).start()

    @pl.loop(0, chunks)
    def _(n):
        for kind in range(7):
            fin_copy(kind, me_s, n, zp).wait_send()
        for j in range(PASSES - 1):
            hi_copy(j, n).wait_send()
            lo_copy(j, n).wait_send()

    for i, block in enumerate((me_s, zp, yp, ym, y2, zp_m, zp_p, zp_2)):
        out_copy(block, i).wait()


def sweep(tiles, chunks, order, mask, start, meas, system):
    subsets, slices, vox = start.shape
    rays = system.shape[1]
    chunk = rays // tiles
    hops = PASSES - 1
    dma = pltpu.SemaphoreType.DMA
    vmem = pl.BlockSpec(memory_space=pltpu.VMEM)
    hbm = pl.BlockSpec(memory_space=pl.ANY)
    return pl.pallas_call(
        functools.partial(sweep_kernel, tiles),
        out_shape=jax.ShapeDtypeStruct((subsets, slices, vox), BF16),
        in_specs=[vmem, vmem, hbm, hbm, hbm],
        out_specs=hbm,
        scratch_shapes=[
            pltpu.VMEM((rays, vox), BF16),
            pltpu.VMEM((subsets, slices, vox), BF16),
            pltpu.VMEM((slices + ONES, vox), BF16),
            pltpu.VMEM((subsets, slices, chunk), BF16),
            pltpu.VMEM((PASSES, slices, chunk), F32),
            pltpu.VMEM((1, chunk), F32),
            pltpu.VMEM((1, vox), F32),
            pltpu.VMEM((tiles, slices + ONES, chunk), BF16),
            pltpu.VMEM((PASSES, tiles, slices + ONES, chunk), BF16),
            pltpu.VMEM((PASSES, slices + ONES, rays), BF16),
            pltpu.VMEM((hops, slices, vox), BF16),
            pltpu.VMEM((hops, slices, vox), BF16),
            pltpu.VMEM((hops, slices, vox), BF16),
            pltpu.VMEM((hops, slices, vox), BF16),
            pltpu.VMEM((slices, rays), F32),
            pltpu.VMEM((subsets, slices, vox), BF16),
            dma((rays // (2 * chunk),)),
            dma((2,)),
            dma((tiles,)),
            dma((PASSES, tiles)),
            dma((tiles,)),
            dma((PASSES, tiles)),
            dma((hops, 2, chunks)),
            dma((hops, 2, chunks)),
            dma((7, chunks)),
            dma((7, chunks)),
            dma((8,)),
        ],
        compiler_params=pltpu.CompilerParams(
            collective_id=0, has_side_effects=True, vmem_limit_bytes=60 * 1024 * 1024
        ),
    )(order, mask, start, meas, system)


def body(tiles, chunks, start_volume, measured, system_values, block_pattern, subset_order):
    subsets, slices, vox = start_volume.shape
    mask = jnp.repeat(block_pattern[0].astype(F32), SIDE, axis=1)
    owners = lax.rem(subset_order + (PASSES - 1), subsets)
    same = jnp.arange(slices)[:, None, None, None] == jnp.arange(slices)[None, None, None, :]
    hit = owners[:, :, None, None] == jnp.arange(subsets)[None, None, :, None]
    pick = jnp.transpose(same & hit, (1, 0, 2, 3)).reshape(subsets * slices, subsets * slices).astype(BF16)
    gathered = sweep(tiles, chunks, subset_order, mask, start_volume, measured, system_values)
    placed = dot(pick, gathered.reshape(subsets * slices, vox), NN)
    return placed.astype(BF16).reshape(start_volume.shape)


def solution(mesh):
    placed = (
        P(None, None, "tile"),
        P("subset", None, None, None),
        P("subset", None, "tile"),
        P("subset", None, "tile"),
        P(),
    )
    return jax.shard_map(
        functools.partial(body, mesh.shape["tile"], 8),
        mesh=mesh, in_specs=placed, out_specs=P(None, None, "tile"), check_vma=False,
    )
```

time: 975 us -> 198 us (0.20); the launches traced: 965 us -> 198 us
  waiting for transfers between devices: 765 us -> 0 us
  Pallas kernels: 0 us -> 186 us
  matrix products: 98.5 us -> 6.54 us
  blocking collectives: 35.4 us -> 0 us
  local copies, waits for them, and re-layouts: 30.7 us -> 3.35 us
  other arithmetic: 19.2 us -> 2.24 us
  between operations: 13.4 us -> 0.04 us
    psum x5 -> x0, waiting for transfers between devices: 688 us -> none  [the longest x4 505 us: body(): projected = lax.psum(partial_value, 'tile')]
    pallas_call x0 -> x1, Pallas kernels: none -> 186 us  [sweep(): pl.pallas_call(functools.partial(sweep_kernel, tiles), out_shape=jax.Shap...]
    dot_general x13 -> x1, matrix products: 98.5 us -> 6.54 us  [dot(): return lax.dot_general(a, b, dims, preferred_element_type=F32)]
    ppermute x3 -> x0, waiting for transfers between devices: 77.3 us -> none  [passed_along(): return lax.ppermute(block, axis, route)]
    psum x1 -> x0, blocking collectives: 35.4 us -> none  [body(): ray_total = lax.psum(row_part, 'tile')]
    broadcast_in_dim x2 -> x1, local copies, waits for them, and re-layouts: 25.5 us -> 0.12 us  [body(): mask = jnp.repeat(block_pattern[0].astype(F32), SIDE, axis=1)]
    reduce_sum x1 -> x0, other arithmetic: 14.5 us -> none  [body(): row_part = jnp.sum(matrix, axis=1, dtype=jnp.float32)[None, :]]
  transfers between devices with their start and end apart: 8 -> 0, of which waited for: 8 -> 0; matrix products, arithmetic and copies ran while one was open for 1% -> 0% of each run, Pallas kernels for 0% -> 0%
where the time goes in v1:
time: 198 us
  Pallas kernels  186 us (94%)
  matrix products  6.54 us (3%)
  local copies, waits for them, and re-layouts  3.35 us (2%)
  other arithmetic  2.24 us (1%)
    pallas_call x1, Pallas kernels, sweep(): pl.pallas_call(functools.partial(sweep_kernel, tiles), out_shape=jax.Shap...  186 us
    dot_general x1, matrix products, dot(): return lax.dot_general(a, b, dims, preferred_element_type=F32)  6.54 us

profile of v1, /device:TPU:1, one launch (start us, length us, event | category | flops | bytes accessed | tf_op | source)
XLA Modules:
  0.0 198.2 jit_solution(241211260987110624)
XLA Ops:
  0.0 0.7 fusion.1
  0.7 0.7 convert_bitcast_fusion
  1.4 1.4 copy.6.order_ref
  2.8 0.1 iota_compare_fusion
  2.9 0.1 broadcast_in_dim.2
  3.0 0.9 copy.9
  3.9 0.7 broadcast_and_fusion
  4.6 1.0 and.28
  5.6 186.0 %shard_map.55 = bf16[8,64,4096]{2,1,0:T(8,128)(2,1)} custom-call(s32[64,8]{1,0:T(8,128)} %copy.6.order_ref, f32[16,4096]{1,0:T(8,128)} %bitcast.15, bf16[8,64,4096]{2,1,0:T(8,128)(2,1)} %start_hbm.1, bf16[1,8,64,2048]{3,2,1,0:T(8,128)(2,1)} %meas_hbm.1, bf16[1,2048,4096]{2,1,0:T(8,128)(2,1)} %sys_hbm.1), custom_call_target="tpu_custom_call" | custom-call | tf_op jit(solution)/shard_map/pallas_call | solution.py:306
  191.7 6.5 %convolution_convert_fusion = bf16[512,4096]{1,0:T(8,128)(2,1)} fusion(pred[512,512]{1,0:T(32,128)(4,1)S(1)} %and.28, bf16[512,4096]{1,0:T(8,128)(2,1)} %bitcast.14), kind=kOutput, calls=%fused_computation | convolution fusion | flops 2149580800 | bytes 8650752 | tf_op jit(solution)/shard_map/dot_general | solution.py:21
  (1 shorter events, 0.0 us)

commit v2 on v1

--- a/solution.py
+++ b/solution.py
@@ -22,10 +22,11 @@
 
 
 def sweep_kernel(
-    tiles, order_ref, mask_ref, start_hbm, meas_hbm, sys_hbm, out_hbm,
-    a_ref, start_ref, vb_ref, meas_ref, dest_ref, rows_ref, inv_ref, part, recv, resid,
-    hi_out, lo_out, hi_in, lo_in, acc, gat,
-    a_sem, io_sem, rs_send, rs_recv, ag_send, ag_recv, hop_send, hop_recv, fin_send, fin_recv, out_sem,
+    tiles, order_hbm, pattern_hbm, start_hbm, meas_hbm, sys_hbm, out_hbm,
+    order_ref, pattern_ref, mask_ref, a_ref, start_ref, vb_ref, meas_ref, dest_ref, rows_ref, inv_ref,
+    part, recv, resid, mid_out, mid_in, hop_out, hop_in, acc, gat,
+    a_sem, io_sem, rs_send, rs_recv, ag_send, ag_recv, mid_send, mid_recv, hop_send, hop_recv,
+    fin_send, fin_recv, out_sem,
 ):
     me_s, me_t = lax.axis_index("subset"), lax.axis_index("tile")
     subsets = order_ref.shape[1]
@@ -34,7 +35,7 @@
     chunk = rays // tiles
     pair = 2 * chunk
     pairs = rays // pair
-    chunks = hop_send.shape[2]
+    chunks = hop_send.shape[1]
     width = vox // chunks
 
     def tile_at(d):
@@ -55,6 +56,10 @@
     def rays_of(c):
         return pl.ds(pl.multiple_of(c * chunk, chunk), chunk)
 
+    order_copy = pltpu.make_async_copy(order_hbm, order_ref, io_sem.at[2])
+    order_copy.start()
+    pattern_copy = pltpu.make_async_copy(pattern_hbm.at[0], pattern_ref, io_sem.at[3])
+    pattern_copy.start()
     start_copy = pltpu.make_async_copy(start_hbm, start_ref, io_sem.at[0])
     start_copy.start()
     half = lax.div(me_t, 2)
@@ -83,15 +88,27 @@
     vb_ref[slices:, :] = jnp.ones((ONES, vox), BF16)
     resid[0, slices:, :] = jnp.ones((ONES, rays), BF16)
 
-    start_copy.wait()
-
-    @pl.loop(0, chunks)
-    def _(n):
+    def select_start(source, n):
         total = jnp.zeros((slices, width), F32)
         for f in range(subsets):
-            weight = (order_ref[:, f : f + 1] == me_s).astype(F32)
+            weight = (order_ref[:, f : f + 1] == source).astype(F32)
             total += weight * start_ref[f, :, cols(n)].astype(F32)
-        vb_ref[:slices, cols(n)] = total.astype(BF16)
+        return total.astype(BF16)
+
+    pattern_copy.wait()
+    blocks = pattern_ref.shape[1]
+    spread = lax.broadcasted_iota(jnp.int32, (blocks, vox), 1) // SIDE == lax.broadcasted_iota(
+        jnp.int32, (blocks, vox), 0
+    )
+    mask_ref[...] = dot(
+        pattern_ref[...].astype(F32).astype(BF16), spread.astype(F32).astype(BF16), NN
+    )
+    order_copy.wait()
+    start_copy.wait()
+
+    @pl.loop(0, chunks)
+    def _(n):
+        vb_ref[:slices, cols(n)] = select_start(me_s, n)
 
     pl.semaphore_wait(barrier, tiles - 1 + subsets - 1)
 
@@ -149,17 +166,22 @@
         here = resid.at[j, pl.ds(0, slices), rays_of(lax.rem(me_t + tiles - d, tiles))]
         return remote(here, here, ag_send.at[d], ag_recv.at[j, d], me_s, tile_at(d))
 
-    def hi_copy(j, n):
+    def hop_copy(j, n):
         return remote(
-            hi_out.at[j, :, cols(n)], hi_in.at[j, :, cols(n)],
-            hop_send.at[j, 0, n], hop_recv.at[j, 0, n], subset_at(1), me_t,
+            hop_out.at[j, :, cols(n)], hop_in.at[j, :, cols(n)],
+            hop_send.at[j, n], hop_recv.at[j, n], subset_at(1), me_t,
         )
 
-    def lo_copy(j, n):
+    def mid_copy(j):
         return remote(
-            lo_out.at[j, :, cols(n)], lo_in.at[j, :, cols(n)],
-            hop_send.at[j, 1, n], hop_recv.at[j, 1, n], subset_at(1), me_t,
+            mid_out.at[j], mid_in.at[j], mid_send.at[j], mid_recv.at[j], subset_at(1), me_t
         )
+
+    def wide(x):
+        return jnp.concatenate([x] * (width // x.shape[1]), axis=1)
+
+    def change_so_far(j, n):
+        return hop_in[j - 1, :, cols(n)].astype(F32) + wide(mid_in[j - 1].astype(F32))
 
     zp = me_s + 1 - 2 * lax.rem(me_s, 2)
     yp, ym, y2 = subset_at(2), subset_at(subsets - 2), subset_at(subsets // 2)
@@ -175,20 +197,23 @@
         height = slices + ONES if j == 0 else slices
         if j > 0:
             acc[...] = jnp.zeros_like(acc)
+            mid_copy(j - 1).wait_recv()
 
             @pl.loop(0, chunks)
             def _(n):
-                hi_copy(j - 1, n).wait_recv()
-                acc[...] += dot(hi_in[j - 1, :, cols(n)], a_ref[:, cols(n)], NT)
+                hop_copy(j - 1, n).wait_recv()
+                volume = vb_ref[:slices, cols(n)].astype(F32) + change_so_far(j, n)
+                acc[...] += dot(volume.astype(BF16), a_ref[:, cols(n)], NT)
 
             for c in range(tiles):
                 part[c, pl.ds(0, slices), :] = acc[:, c * chunk : (c + 1) * chunk].astype(BF16)
             for d in range(1, tiles):
                 rs_copy(j, d, tile_at(d), slices).start()
 
-            @pl.loop(0, chunks // 2)
+        if j + 1 < PASSES:
+            @pl.loop(0, chunks)
             def _(n):
-                lo_copy(j - 1, n).start()
+                vb_ref[:slices, cols(n)] = select_start(lax.rem(me_s + subsets - j - 1, subsets), n)
 
         total = part[me_t].astype(F32) if j == 0 else part[me_t, pl.ds(0, slices), :].astype(F32)
         for d in range(1, tiles):
@@ -200,10 +225,6 @@
         resid[j, pl.ds(0, slices), rays_of(me_t)] = value.astype(BF16)
         for d in range(1, tiles):
             ag_copy(j, d).start()
-        if j > 0:
-            @pl.loop(chunks // 2, chunks)
-            def _(n):
-                lo_copy(j - 1, n).start()
         for d in range(1, tiles):
             rs_copy(j, d, tile_at(d), height).wait_send()
         for d in range(1, tiles):
@@ -216,20 +237,21 @@
                 back = dot(resid[0], a_ref[:, here], NN)
                 inv = 1.0 / back[slices : slices + 1, :]
                 inv_ref[:, here] = inv
-                base = vb_ref[:slices, here].astype(F32)
+                change = back[:slices, :] * inv
             else:
                 back = dot(resid[j, pl.ds(0, slices), :], a_ref[:, here], NN)
-                inv = inv_ref[:, here]
-                lo_copy(j - 1, n).wait_recv()
-                base = hi_in[j - 1, :, here].astype(F32) + lo_in[j - 1, :, here].astype(F32)
-            volume = base + back[:slices, :] * inv
-            high = volume.astype(BF16)
+                change = change_so_far(j, n) + back * inv_ref[:, here]
             if j + 1 < PASSES:
-                hi_out[j, :, here] = high
-                lo_out[j, :, here] = (volume - high.astype(F32)).astype(BF16)
-                hi_copy(j, n).start()
+                @pl.when(n == 0)
+                def _():
+                    mean = jnp.sum(change, axis=1, keepdims=True) * (1.0 / width)
+                    mid_out[j] = jnp.broadcast_to(mean, mid_out.shape[1:]).astype(BF16)
+                    mid_copy(j).start()
+
+                hop_out[j, :, here] = (change - wide(mid_out[j].astype(F32))).astype(BF16)
+                hop_copy(j, n).start()
             else:
-                gat[me_s, :, here] = high
+                gat[me_s, :, here] = (vb_ref[:slices, here].astype(F32) + change).astype(BF16)
                 fin_copy(0, me_s, n, zp).start()
                 fin_copy(1, me_s, n, yp).start()
                 fin_copy(2, me_s, n, ym).start()
@@ -288,27 +310,31 @@
         for kind in range(7):
             fin_copy(kind, me_s, n, zp).wait_send()
         for j in range(PASSES - 1):
-            hi_copy(j, n).wait_send()
-            lo_copy(j, n).wait_send()
+            hop_copy(j, n).wait_send()
+
+    for j in range(PASSES - 1):
+        mid_copy(j).wait_send()
 
     for i, block in enumerate((me_s, zp, yp, ym, y2, zp_m, zp_p, zp_2)):
         out_copy(block, i).wait()
 
 
-def sweep(tiles, chunks, order, mask, start, meas, system):
+def sweep(tiles, chunks, order, pattern, start, meas, system):
     subsets, slices, vox = start.shape
     rays = system.shape[1]
     chunk = rays // tiles
     hops = PASSES - 1
     dma = pltpu.SemaphoreType.DMA
-    vmem = pl.BlockSpec(memory_space=pltpu.VMEM)
     hbm = pl.BlockSpec(memory_space=pl.ANY)
     return pl.pallas_call(
         functools.partial(sweep_kernel, tiles),
         out_shape=jax.ShapeDtypeStruct((subsets, slices, vox), BF16),
-        in_specs=[vmem, vmem, hbm, hbm, hbm],
+        in_specs=[hbm] * 5,
         out_specs=hbm,
         scratch_shapes=[
+            pltpu.VMEM(order.shape, jnp.int32),
+            pltpu.VMEM(pattern.shape[1:], jnp.int32),
+            pltpu.VMEM((pattern.shape[1], vox), F32),
             pltpu.VMEM((rays, vox), BF16),
             pltpu.VMEM((subsets, slices, vox), BF16),
             pltpu.VMEM((slices + ONES, vox), BF16),
@@ -319,20 +345,22 @@
             pltpu.VMEM((tiles, slices + ONES, chunk), BF16),
             pltpu.VMEM((PASSES, tiles, slices + ONES, chunk), BF16),
             pltpu.VMEM((PASSES, slices + ONES, rays), BF16),
-            pltpu.VMEM((hops, slices, vox), BF16),
-            pltpu.VMEM((hops, slices, vox), BF16),
+            pltpu.VMEM((hops, slices, SIDE), BF16),
+            pltpu.VMEM((hops, slices, SIDE), BF16),
             pltpu.VMEM((hops, slices, vox), BF16),
             pltpu.VMEM((hops, slices, vox), BF16),
             pltpu.VMEM((slices, rays), F32),
             pltpu.VMEM((subsets, slices, vox), BF16),
             dma((rays // (2 * chunk),)),
-            dma((2,)),
+            dma((4,)),
             dma((tiles,)),
             dma((PASSES, tiles)),
             dma((tiles,)),
             dma((PASSES, tiles)),
-            dma((hops, 2, chunks)),
-            dma((hops, 2, chunks)),
+            dma((hops,)),
+            dma((hops,)),
+            dma((hops, chunks)),
+            dma((hops, chunks)),
             dma((7, chunks)),
             dma((7, chunks)),
             dma((8,)),
@@ -340,19 +368,49 @@
         compiler_params=pltpu.CompilerParams(
             collective_id=0, has_side_effects=True, vmem_limit_bytes=60 * 1024 * 1024
         ),
-    )(order, mask, start, meas, system)
+    )(order, pattern, start, meas, system)
+
+
+def place_kernel(order_ref, gathered_ref, out_ref, pick_ref):
+    fronts, slices, width = gathered_ref.shape
+    half = slices // 2
+    side = fronts * half
+
+    @pl.when(pl.program_id(0) == 0)
+    def _():
+        column = lax.broadcasted_iota(jnp.int32, (half, side), 1)
+        row = lax.broadcasted_iota(jnp.int32, (half, side), 0)
+        for h in range(2):
+            for f in range(fronts):
+                owner = lax.rem(order_ref[h * half : (h + 1) * half, f : f + 1] + (PASSES - 1), fronts)
+                hit = column == owner * half + row
+                pick_ref[h, f * half : (f + 1) * half, :] = hit.astype(F32).astype(BF16)
+
+    for h in range(2):
+        rows = gathered_ref[:, h * half : (h + 1) * half, :].reshape(side, width)
+        placed = dot(pick_ref[h], rows, NN).astype(BF16)
+        out_ref[:, h * half : (h + 1) * half, :] = placed.reshape(fronts, half, width)
+
+
+def place(order, gathered, steps):
+    fronts, slices, vox = gathered.shape
+    block = pl.BlockSpec((fronts, slices, vox // steps), lambda n: (0, 0, n))
+    side = fronts * slices // 2
+    return pl.pallas_call(
+        place_kernel,
+        out_shape=jax.ShapeDtypeStruct(gathered.shape, BF16),
+        grid=(steps,),
+        in_specs=[pl.BlockSpec(order.shape, lambda n: (0, 0)), block],
+        out_specs=block,
+        scratch_shapes=[pltpu.VMEM((2, side, side), BF16)],
+    )(order, gathered)
 
 
 def body(tiles, chunks, start_volume, measured, system_values, block_pattern, subset_order):
-    subsets, slices, vox = start_volume.shape
-    mask = jnp.repeat(block_pattern[0].astype(F32), SIDE, axis=1)
-    owners = lax.rem(subset_order + (PASSES - 1), subsets)
-    same = jnp.arange(slices)[:, None, None, None] == jnp.arange(slices)[None, None, None, :]
-    hit = owners[:, :, None, None] == jnp.arange(subsets)[None, None, :, None]
-    pick = jnp.transpose(same & hit, (1, 0, 2, 3)).reshape(subsets * slices, subsets * slices).astype(BF16)
-    gathered = sweep(tiles, chunks, subset_order, mask, start_volume, measured, system_values)
-    placed = dot(pick, gathered.reshape(subsets * slices, vox), NN)
-    return placed.astype(BF16).reshape(start_volume.shape)
+    gathered = sweep(
+        tiles, chunks, subset_order, block_pattern, start_volume, measured, system_values
+    )
+    return place(subset_order, gathered, 8)
 
 
 def solution(mesh):

time: 198 us -> 157 us (0.79)
  Pallas kernels: 186 us -> 155 us
  matrix products: 6.54 us -> 0 us
  other arithmetic: 2.24 us -> 0 us
  local copies, waits for them, and re-layouts: 3.35 us -> 1.37 us
    pallas_call x1, Pallas kernels: 186 us -> 147 us  [sweep(): pl.pallas_call(functools.partial(sweep_kernel, tiles), out_shape=jax.Shap...]
    pallas_call x0 -> x1, Pallas kernels: none -> 7.69 us  [place(): pl.pallas_call(place_kernel, out_shape=jax.ShapeDtypeStruct(gathered.shap...]
    dot_general x1 -> x0, matrix products: 6.54 us -> none  [dot(): return lax.dot_general(a, b, dims, preferred_element_type=F32)]
where the time goes in v2:
time: 157 us; the launch traced here: 156 us
  Pallas kernels  155 us (99%)
    pallas_call x1, Pallas kernels, sweep(): pl.pallas_call(functools.partial(sweep_kernel, tiles), out_shape=jax.Shap...  147 us
    pallas_call x1, Pallas kernels, place(): pl.pallas_call(place_kernel, out_shape=jax.ShapeDtypeStruct(gathered.shap...  7.69 us

profile of v2, /device:TPU:1, one launch (start us, length us, event | category | flops | bytes accessed | tf_op | source)
XLA Modules:
  0.0 156.3 jit_solution(2606542369928304742)
XLA Ops:
  0.0 1.4 copy.7.order_hbm.order_ref
  1.4 147.3 %shard_map.55.gathered_ref = bf16[8,64,4096]{2,1,0:T(8,128)(2,1)} custom-call(s32[64,8]{1,0:T(8,128)} %copy.7.order_hbm.order_ref, s32[1,16,32]{2,1,0:T(8,128)} %pattern_hbm.1, bf16[8,64,4096]{2,1,0:T(8,128)(2,1)} %start_hbm.1, bf16[1,8,64,2048]{3,2,1,0:T(8,128)(2,1)} %meas_hbm.1, bf16[1,2048,4096]{2,1,0:T(8,128)(2,1)} %sys_hbm.1), custom_call_target="tpu_custom_call" | custom-call | tf_op jit(solution)/shard_map/pallas_call | solution.py:329
  148.6 7.7 %shard_map.56 = bf16[8,64,4096]{2,1,0:T(8,128)(2,1)} custom-call(s32[64,8]{1,0:T(8,128)} %copy.7.order_hbm.order_ref, bf16[8,64,4096]{2,1,0:T(8,128)(2,1)} %shard_map.55.gathered_ref), custom_call_target="tpu_custom_call" | custom-call | tf_op jit(solution)/shard_map/pallas_call | solution.py:399

commit v3 on v2

--- a/solution.py
+++ b/solution.py
@@ -17,13 +17,32 @@
 NN = (((1,), (0,)), ((), ()))
 
 
+TN = (((0,), (0,)), ((), ()))
+LATE = 3
+
+
+def bit(x, k):
+    return lax.rem(lax.div(x, 2**k), 2)
+
+
+def flip(x, d):
+    for k in range(d.bit_length()):
+        if d >> k & 1:
+            x = x + 2**k * (1 - 2 * bit(x, k))
+    return x
+
+
+def differ(x, y, bits):
+    return sum(2**k * lax.rem(bit(x, k) + bit(y, k), 2) for k in range(bits))
+
+
 def dot(a, b, dims):
     return lax.dot_general(a, b, dims, preferred_element_type=F32)
 
 
 def sweep_kernel(
     tiles, order_hbm, pattern_hbm, start_hbm, meas_hbm, sys_hbm, out_hbm,
-    order_ref, pattern_ref, mask_ref, a_ref, start_ref, vb_ref, meas_ref, dest_ref, rows_ref, inv_ref,
+    turned_ref, order_ref, pick_ref, pattern_ref, mask_ref, a_ref, start_ref, vb_ref, meas_ref, dest_ref, rows_ref, inv_ref,
     part, recv, resid, mid_out, mid_in, hop_out, hop_in, acc, gat,
     a_sem, io_sem, rs_send, rs_recv, ag_send, ag_recv, mid_send, mid_recv, hop_send, hop_recv,
     fin_send, fin_recv, out_sem,
@@ -31,6 +50,8 @@
     me_s, me_t = lax.axis_index("subset"), lax.axis_index("tile")
     subsets = order_ref.shape[1]
     slices = order_ref.shape[0]
+    bits = (tiles - 1).bit_length()
+    partners = sorted(range(1, tiles), key=lambda d: -(4 * (d >> 3) + 2 * (d >> 2 & 1) * (1 - (d >> 1 & 1)) + (d >> 1 & 1)))
     rays, vox = a_ref.shape
     chunk = rays // tiles
     pair = 2 * chunk
@@ -39,7 +60,7 @@
     width = vox // chunks
 
     def tile_at(d):
-        return lax.rem(me_t + d, tiles)
+        return flip(me_t, d)
 
     def subset_at(d):
         return lax.rem(me_s + d, subsets)
@@ -56,7 +77,7 @@
     def rays_of(c):
         return pl.ds(pl.multiple_of(c * chunk, chunk), chunk)
 
-    order_copy = pltpu.make_async_copy(order_hbm, order_ref, io_sem.at[2])
+    order_copy = pltpu.make_async_copy(order_hbm, turned_ref, io_sem.at[2])
     order_copy.start()
     pattern_copy = pltpu.make_async_copy(pattern_hbm.at[0], pattern_ref, io_sem.at[3])
     pattern_copy.start()
@@ -64,8 +85,11 @@
     start_copy.start()
     half = lax.div(me_t, 2)
 
+    def pair_at(i):
+        return flip(differ(half, i, bits), max(pairs - 2, 0))
+
     def block_rows(i):
-        return pl.ds(pl.multiple_of(lax.rem(half + i, pairs) * pair, pair), pair)
+        return pl.ds(pl.multiple_of(pair_at(i) * pair, pair), pair)
 
     def matrix_copy(i):
         return pltpu.make_async_copy(
@@ -88,12 +112,24 @@
     vb_ref[slices:, :] = jnp.ones((ONES, vox), BF16)
     resid[0, slices:, :] = jnp.ones((ONES, rays), BF16)
 
-    def select_start(source, n):
-        total = jnp.zeros((slices, width), F32)
-        for f in range(subsets):
-            weight = (order_ref[:, f : f + 1] == source).astype(F32)
-            total += weight * start_ref[f, :, cols(n)].astype(F32)
-        return total.astype(BF16)
+    def wide(x):
+        return jnp.concatenate([x] * (width // x.shape[1]), axis=1)
+
+    def hits(source):
+        return [
+            jnp.broadcast_to((order_ref[:, f : f + 1] == source).astype(F32), (slices, SIDE)).astype(BF16)
+            for f in range(subsets)
+        ]
+
+    def select_start(source):
+        weights = hits(source)
+
+        @pl.loop(0, chunks)
+        def _(n):
+            total = wide(weights[0]) * start_ref[0, :, cols(n)]
+            for f in range(1, subsets):
+                total += wide(weights[f]) * start_ref[f, :, cols(n)]
+            vb_ref[:slices, cols(n)] = total
 
     pattern_copy.wait()
     blocks = pattern_ref.shape[1]
@@ -104,31 +140,39 @@
         pattern_ref[...].astype(F32).astype(BF16), spread.astype(F32).astype(BF16), NN
     )
     order_copy.wait()
+    same = lax.broadcasted_iota(jnp.int32, (subsets, subsets), 0) == lax.broadcasted_iota(
+        jnp.int32, (subsets, subsets), 1
+    )
+    order_ref[...] = dot(
+        turned_ref[...].astype(F32).astype(BF16), same.astype(F32).astype(BF16), TN
+    ).astype(jnp.int32)
     start_copy.wait()
-
-    @pl.loop(0, chunks)
-    def _(n):
-        vb_ref[:slices, cols(n)] = select_start(me_s, n)
+    select_start(me_s)
 
     pl.semaphore_wait(barrier, tiles - 1 + subsets - 1)
 
     def rs_copy(j, d, c, height):
         return remote(
             part.at[c, pl.ds(0, height), :], recv.at[j, d, pl.ds(0, height), :],
-            rs_send.at[d], rs_recv.at[j, d], me_s, tile_at(d),
+            rs_send.at[d], rs_recv.at[j, d], me_s, c,
         )
 
     @pl.loop(0, pairs)
     def _(i):
         matrix_copy(i).wait()
-        b = lax.rem(half + i, pairs)
+        b = pair_at(i)
         per_pair = pair // SIDE
-        for q in range(per_pair):
-            mask = jnp.broadcast_to(mask_ref[pl.ds(b * per_pair + q, 1), :], (16, vox)).astype(BF16)
-            for u in range(SIDE // 16):
-                here = pl.ds(pl.multiple_of(b * pair + q * SIDE + u * 16, 16), 16)
-                a_ref[here, :] = a_ref[here, :] * mask
-        p = dot(vb_ref[...], a_ref[block_rows(i), :], NT)
+        piece = min(512, vox)
+        p = jnp.zeros((slices + ONES, pair), F32)
+        for k in range(0, vox, piece):
+            parts = []
+            for q in range(per_pair):
+                mask = jnp.broadcast_to(mask_ref[pl.ds(b * per_pair + q, 1), k : k + piece], (16, piece)).astype(BF16)
+                here = pl.ds(pl.multiple_of(b * pair + q * SIDE, SIDE), SIDE)
+                masked = a_ref[here, k : k + piece] * jnp.concatenate([mask] * (SIDE // 16), axis=0)
+                a_ref[here, k : k + piece] = masked
+                parts.append(masked)
+            p += dot(vb_ref[:, k : k + piece], jnp.concatenate(parts, axis=0), NT)
         sums = p[slices:, :]
         high = sums.astype(BF16)
         rest = sums - high.astype(F32)
@@ -143,11 +187,21 @@
             c = 2 * b + h
             part[c, pl.ds(0, slices), :] = p[:slices, h * chunk : (h + 1) * chunk].astype(BF16)
             part[c, pl.ds(slices, ONES), :] = packed[:, h * chunk : (h + 1) * chunk]
-            d = lax.rem(c + tiles - me_t, tiles)
+            d = differ(c, me_t, bits)
 
             @pl.when(d != 0)
             def _():
                 rs_copy(0, d, c, slices + ONES).start()
+
+    half_slices = slices // 2
+    side = subsets * half_slices
+    column = lax.broadcasted_iota(jnp.int32, (half_slices, side), 1)
+    row = lax.broadcasted_iota(jnp.int32, (half_slices, side), 0)
+    for h in range(2):
+        for f in range(subsets):
+            last = lax.rem(order_ref[h * half_slices : (h + 1) * half_slices, f : f + 1] + (PASSES - 1), subsets)
+            hit = column == last * half_slices + row
+            pick_ref[h, f * half_slices : (f + 1) * half_slices, :] = hit.astype(F32).astype(BF16)
 
     meas_copy.wait()
     for j in range(PASSES):
@@ -163,7 +217,7 @@
         return remote(here, here, ag_send.at[d], ag_recv.at[j, d], me_s, tile_at(d))
 
     def ag_arrival(j, d):
-        here = resid.at[j, pl.ds(0, slices), rays_of(lax.rem(me_t + tiles - d, tiles))]
+        here = resid.at[j, pl.ds(0, slices), rays_of(tile_at(d))]
         return remote(here, here, ag_send.at[d], ag_recv.at[j, d], me_s, tile_at(d))
 
     def hop_copy(j, n):
@@ -177,9 +231,6 @@
             mid_out.at[j], mid_in.at[j], mid_send.at[j], mid_recv.at[j], subset_at(1), me_t
         )
 
-    def wide(x):
-        return jnp.concatenate([x] * (width // x.shape[1]), axis=1)
-
     def change_so_far(j, n):
         return hop_in[j - 1, :, cols(n)].astype(F32) + wide(mid_in[j - 1].astype(F32))
 
@@ -207,23 +258,21 @@
 
             for c in range(tiles):
                 part[c, pl.ds(0, slices), :] = acc[:, c * chunk : (c + 1) * chunk].astype(BF16)
-            for d in range(1, tiles):
+            for d in partners:
                 rs_copy(j, d, tile_at(d), slices).start()
 
         if j + 1 < PASSES:
-            @pl.loop(0, chunks)
-            def _(n):
-                vb_ref[:slices, cols(n)] = select_start(lax.rem(me_s + subsets - j - 1, subsets), n)
+            select_start(lax.rem(me_s + subsets - j - 1, subsets))
 
         total = part[me_t].astype(F32) if j == 0 else part[me_t, pl.ds(0, slices), :].astype(F32)
-        for d in range(1, tiles):
+        for d in reversed(partners):
             rs_copy(j, d, tile_at(d), height).wait_recv()
             total += recv[j, d, pl.ds(0, height), :].astype(F32)
         if j == 0:
             rows_ref[...] = jnp.sum(total[slices:, :], axis=0, keepdims=True)
         value = (dest_ref[j] - total[:slices, :]) / rows_ref[...]
         resid[j, pl.ds(0, slices), rays_of(me_t)] = value.astype(BF16)
-        for d in range(1, tiles):
+        for d in partners:
             ag_copy(j, d).start()
         for d in range(1, tiles):
             rs_copy(j, d, tile_at(d), height).wait_send()
@@ -259,6 +308,8 @@
         for d in range(1, tiles):
             ag_copy(j, d).wait_send()
 
+    late = min(LATE, chunks - 1)
+
     @pl.loop(0, chunks)
     def _(n):
         fin_copy(1, ym, n, me_s).wait_recv()
@@ -272,51 +323,69 @@
         def _():
             fin_copy(3, yp, n, ym).start()
 
+        @pl.when(n < late)
+        def _():
+            fin_copy(7, ym, n, zp).start()
+            fin_copy(8, yp, n, zp).start()
+
     @pl.loop(0, chunks)
     def _(n):
         fin_copy(0, zp, n, me_s).wait_recv()
-        fin_copy(4, zp, n, yp).start()
-        fin_copy(5, zp, n, ym).start()
-
-    def out_copy(block, i):
-        return pltpu.make_async_copy(gat.at[block], out_hbm.at[block], out_sem.at[i])
-
-    for i, block in enumerate((me_s, zp, yp, ym)):
-        out_copy(block, i).start()
+
+        @pl.when(n >= late)
+        def _():
+            fin_copy(4, zp, n, yp).start()
+            fin_copy(5, zp, n, ym).start()
 
     @pl.loop(0, chunks)
     def _(n):
         fin_copy(3, y2, n, me_s).wait_recv()
         fin_copy(6, y2, n, zp).start()
 
-    out_copy(y2, 4).start()
+    def out_copy(n):
+        return pltpu.make_async_copy(start_ref.at[:, :, cols(n)], out_hbm.at[:, :, cols(n)], out_sem.at[n])
 
     @pl.loop(0, chunks)
     def _(n):
-        fin_copy(4, zp_m, n, me_s).wait_recv()
-        fin_copy(5, zp_p, n, me_s).wait_recv()
-
-    out_copy(zp_m, 5).start()
-    out_copy(zp_p, 6).start()
+        @pl.when(n < late)
+        def _():
+            fin_copy(7, zp_m, n, me_s).wait_recv()
+            fin_copy(8, zp_p, n, me_s).wait_recv()
+
+        @pl.when(n >= late)
+        def _():
+            fin_copy(4, zp_m, n, me_s).wait_recv()
+            fin_copy(5, zp_p, n, me_s).wait_recv()
+
+        fin_copy(6, zp_2, n, me_s).wait_recv()
+        for h in range(2):
+            there = pl.ds(h * half_slices, half_slices)
+            rows = gat[:, there, cols(n)].reshape(side, width)
+            placed = dot(pick_ref[h], rows, NN).astype(BF16)
+            start_ref[:, there, cols(n)] = placed.reshape(subsets, half_slices, width)
+        out_copy(n).start()
 
     @pl.loop(0, chunks)
     def _(n):
-        fin_copy(6, zp_2, n, me_s).wait_recv()
-
-    out_copy(zp_2, 7).start()
-
-    @pl.loop(0, chunks)
-    def _(n):
-        for kind in range(7):
+        for kind in (0, 1, 2, 3, 6):
             fin_copy(kind, me_s, n, zp).wait_send()
+
+        @pl.when(n < late)
+        def _():
+            fin_copy(7, me_s, n, zp).wait_send()
+            fin_copy(8, me_s, n, zp).wait_send()
+
+        @pl.when(n >= late)
+        def _():
+            fin_copy(4, me_s, n, zp).wait_send()
+            fin_copy(5, me_s, n, zp).wait_send()
+
         for j in range(PASSES - 1):
             hop_copy(j, n).wait_send()
+        out_copy(n).wait()
 
     for j in range(PASSES - 1):
         mid_copy(j).wait_send()
-
-    for i, block in enumerate((me_s, zp, yp, ym, y2, zp_m, zp_p, zp_2)):
-        out_copy(block, i).wait()
 
 
 def sweep(tiles, chunks, order, pattern, start, meas, system):
@@ -333,6 +402,8 @@
         out_specs=hbm,
         scratch_shapes=[
             pltpu.VMEM(order.shape, jnp.int32),
+            pltpu.VMEM(order.shape[::-1], jnp.int32),
+            pltpu.VMEM((2, subsets * slices // 2, subsets * slices // 2), BF16),
             pltpu.VMEM(pattern.shape[1:], jnp.int32),
             pltpu.VMEM((pattern.shape[1], vox), F32),
             pltpu.VMEM((rays, vox), BF16),
@@ -361,9 +432,9 @@
             dma((hops,)),
             dma((hops, chunks)),
             dma((hops, chunks)),
-            dma((7, chunks)),
-            dma((7, chunks)),
-            dma((8,)),
+            dma((9, chunks)),
+            dma((9, chunks)),
+            dma((chunks,)),
         ],
         compiler_params=pltpu.CompilerParams(
             collective_id=0, has_side_effects=True, vmem_limit_bytes=60 * 1024 * 1024
@@ -371,46 +442,10 @@
     )(order, pattern, start, meas, system)
 
 
-def place_kernel(order_ref, gathered_ref, out_ref, pick_ref):
-    fronts, slices, width = gathered_ref.shape
-    half = slices // 2
-    side = fronts * half
-
-    @pl.when(pl.program_id(0) == 0)
-    def _():
-        column = lax.broadcasted_iota(jnp.int32, (half, side), 1)
-        row = lax.broadcasted_iota(jnp.int32, (half, side), 0)
-        for h in range(2):
-            for f in range(fronts):
-                owner = lax.rem(order_ref[h * half : (h + 1) * half, f : f + 1] + (PASSES - 1), fronts)
-                hit = column == owner * half + row
-                pick_ref[h, f * half : (f + 1) * half, :] = hit.astype(F32).astype(BF16)
-
-    for h in range(2):
-        rows = gathered_ref[:, h * half : (h + 1) * half, :].reshape(side, width)
-        placed = dot(pick_ref[h], rows, NN).astype(BF16)
-        out_ref[:, h * half : (h + 1) * half, :] = placed.reshape(fronts, half, width)
-
-
-def place(order, gathered, steps):
-    fronts, slices, vox = gathered.shape
-    block = pl.BlockSpec((fronts, slices, vox // steps), lambda n: (0, 0, n))
-    side = fronts * slices // 2
-    return pl.pallas_call(
-        place_kernel,
-        out_shape=jax.ShapeDtypeStruct(gathered.shape, BF16),
-        grid=(steps,),
-        in_specs=[pl.BlockSpec(order.shape, lambda n: (0, 0)), block],
-        out_specs=block,
-        scratch_shapes=[pltpu.VMEM((2, side, side), BF16)],
-    )(order, gathered)
-
-
 def body(tiles, chunks, start_volume, measured, system_values, block_pattern, subset_order):
-    gathered = sweep(
-        tiles, chunks, subset_order, block_pattern, start_volume, measured, system_values
-    )
-    return place(subset_order, gathered, 8)
+    return sweep(
+        tiles, chunks, jnp.transpose(subset_order), block_pattern, start_volume, measured, system_values
+    )
 
 
 def solution(mesh):
@@ -422,6 +457,6 @@
         P(),
     )
     return jax.shard_map(
-        functools.partial(body, mesh.shape["tile"], 8),
+        functools.partial(body, mesh.shape["tile"], 16),
         mesh=mesh, in_specs=placed, out_specs=P(None, None, "tile"), check_vma=False,
     )

time: 157 us -> 145 us (0.924)
  Pallas kernels: 155 us -> 140 us
  local copies, waits for them, and re-layouts: 1.37 us -> 4.7 us
    pallas_call x1 -> x0, Pallas kernels: 7.69 us -> none  [place(): pl.pallas_call(place_kernel, out_shape=jax.ShapeDtypeStruct(gathered.shap...]
    pallas_call x1, Pallas kernels: 147 us -> 140 us  [sweep(): pl.pallas_call(functools.partial(sweep_kernel, tiles), out_shape=jax.Shap...]
    unnamed x1, local copies, waits for them, and re-layouts: 1.37 us -> 4.7 us
where the time goes in v3:
time: 145 us
  Pallas kernels  140 us (97%)
  local copies, waits for them, and re-layouts  4.7 us (3%)
    pallas_call x1, Pallas kernels, sweep(): pl.pallas_call(functools.partial(sweep_kernel, tiles), out_shape=jax.Shap...  140 us
    unnamed x1, local copies, waits for them, and re-layouts  4.7 us

profile of v3, /device:TPU:1, one launch (start us, length us, event | category | flops | bytes accessed | tf_op | source)
XLA Modules:
  0.0 144.7 jit_solution(16919786332800446477)
XLA Ops:
  0.0 140.0 %shard_map.55 = bf16[8,64,4096]{2,1,0:T(8,128)(2,1)} custom-call(s32[8,64]{1,0:T(8,128)} %bitcast.1, s32[1,16,32]{2,1,0:T(8,128)} %pattern_hbm.1, bf16[8,64,4096]{2,1,0:T(8,128)(2,1)} %start_hbm.1, bf16[1,8,64,2048]{3,2,1,0:T(8,128)(2,1)} %meas_hbm.1, bf16[1,2048,4096]{2,1,0:T(8,128)(2,1)} %sys_hbm.1), custom_call_target="tpu_custom_call" | custom-call | tf_op jit(solution)/shard_map/pallas_call | solution.py:398
  140.0 4.7 %copy.7 = bf16[8,64,4096]{2,1,0:T(8,128)(2,1)} copy(bf16[8,64,4096]{2,1,0:T(8,128)(2,1)} %shard_map.55) | data formatting | bytes 8388608

commit v4 on v3

--- a/solution.py
+++ b/solution.py
@@ -19,6 +19,9 @@
 
 TN = (((0,), (0,)), ((), ()))
 LATE = 3
+GROUP = 4
+PIECE = 512
+VMEM_LIMIT = 44 * 1024 * 1024
 
 
 def bit(x, k):
@@ -41,11 +44,11 @@
 
 
 def sweep_kernel(
-    tiles, order_hbm, pattern_hbm, start_hbm, meas_hbm, sys_hbm, out_hbm,
+    tiles, order_hbm, pattern_hbm, start_hbm, meas_hbm, sys_hbm, out_ref,
     turned_ref, order_ref, pick_ref, pattern_ref, mask_ref, a_ref, start_ref, vb_ref, meas_ref, dest_ref, rows_ref, inv_ref,
     part, recv, resid, mid_out, mid_in, hop_out, hop_in, acc, gat,
     a_sem, io_sem, rs_send, rs_recv, ag_send, ag_recv, mid_send, mid_recv, hop_send, hop_recv,
-    fin_send, fin_recv, out_sem,
+    fin_send, fin_recv,
 ):
     me_s, me_t = lax.axis_index("subset"), lax.axis_index("tile")
     subsets = order_ref.shape[1]
@@ -54,10 +57,13 @@
     partners = sorted(range(1, tiles), key=lambda d: -(4 * (d >> 3) + 2 * (d >> 2 & 1) * (1 - (d >> 1 & 1)) + (d >> 1 & 1)))
     rays, vox = a_ref.shape
     chunk = rays // tiles
-    pair = 2 * chunk
+    pair = GROUP * chunk
     pairs = rays // pair
     chunks = hop_send.shape[1]
     width = vox // chunks
+
+    chips = [d for d in partners if d % 2 == 0]
+    others = [d + 1 for d in chips] + [1]
 
     def tile_at(d):
         return flip(me_t, d)
@@ -83,7 +89,7 @@
     pattern_copy.start()
     start_copy = pltpu.make_async_copy(start_hbm, start_ref, io_sem.at[0])
     start_copy.start()
-    half = lax.div(me_t, 2)
+    half = lax.div(me_t, GROUP)
 
     def pair_at(i):
         return flip(differ(half, i, bits), max(pairs - 2, 0))
@@ -151,9 +157,10 @@
 
     pl.semaphore_wait(barrier, tiles - 1 + subsets - 1)
 
-    def rs_copy(j, d, c, height):
+    def rs_copy(j, d, c, height, block=None):
+        block = c if block is None else block
         return remote(
-            part.at[c, pl.ds(0, height), :], recv.at[j, d, pl.ds(0, height), :],
+            part.at[block, pl.ds(0, height), :], recv.at[j, d, pl.ds(0, height), :],
             rs_send.at[d], rs_recv.at[j, d], me_s, c,
         )
 
@@ -162,7 +169,7 @@
         matrix_copy(i).wait()
         b = pair_at(i)
         per_pair = pair // SIDE
-        piece = min(512, vox)
+        piece = min(PIECE, vox)
         p = jnp.zeros((slices + ONES, pair), F32)
         for k in range(0, vox, piece):
             parts = []
@@ -183,8 +190,8 @@
             row == 0, high.astype(F32),
             jnp.where(row == 1, mid.astype(F32), jnp.where(row == 2, low.astype(F32), 0.0)),
         ).astype(BF16)
-        for h in range(2):
-            c = 2 * b + h
+        for h in range(GROUP):
+            c = GROUP * b + h
             part[c, pl.ds(0, slices), :] = p[:slices, h * chunk : (h + 1) * chunk].astype(BF16)
             part[c, pl.ds(slices, ONES), :] = packed[:, h * chunk : (h + 1) * chunk]
             d = differ(c, me_t, bits)
@@ -256,16 +263,24 @@
                 volume = vb_ref[:slices, cols(n)].astype(F32) + change_so_far(j, n)
                 acc[...] += dot(volume.astype(BF16), a_ref[:, cols(n)], NT)
 
-            for c in range(tiles):
-                part[c, pl.ds(0, slices), :] = acc[:, c * chunk : (c + 1) * chunk].astype(BF16)
-            for d in partners:
+            for d in others:
+                part[tile_at(d), pl.ds(0, slices), :] = acc[:, rays_of(tile_at(d))].astype(BF16)
+                rs_copy(j, d, tile_at(1), slices, tile_at(d)).start()
+            for d in chips:
+                rs_copy(j, d + 1, tile_at(1), slices).wait_recv()
+                both = acc[:, rays_of(tile_at(d))] + recv[j, d + 1, pl.ds(0, slices), :].astype(F32)
+                part[tile_at(d), pl.ds(0, slices), :] = both.astype(BF16)
                 rs_copy(j, d, tile_at(d), slices).start()
 
         if j + 1 < PASSES:
             select_start(lax.rem(me_s + subsets - j - 1, subsets))
 
-        total = part[me_t].astype(F32) if j == 0 else part[me_t, pl.ds(0, slices), :].astype(F32)
-        for d in reversed(partners):
+        if j == 0:
+            total = part[me_t].astype(F32)
+        else:
+            rs_copy(j, 1, tile_at(1), slices).wait_recv()
+            total = acc[:, rays_of(me_t)] + recv[j, 1, pl.ds(0, slices), :].astype(F32)
+        for d in reversed(partners if j == 0 else chips):
             rs_copy(j, d, tile_at(d), height).wait_recv()
             total += recv[j, d, pl.ds(0, height), :].astype(F32)
         if j == 0:
@@ -342,9 +357,6 @@
         fin_copy(3, y2, n, me_s).wait_recv()
         fin_copy(6, y2, n, zp).start()
 
-    def out_copy(n):
-        return pltpu.make_async_copy(start_ref.at[:, :, cols(n)], out_hbm.at[:, :, cols(n)], out_sem.at[n])
-
     @pl.loop(0, chunks)
     def _(n):
         @pl.when(n < late)
@@ -362,8 +374,7 @@
             there = pl.ds(h * half_slices, half_slices)
             rows = gat[:, there, cols(n)].reshape(side, width)
             placed = dot(pick_ref[h], rows, NN).astype(BF16)
-            start_ref[:, there, cols(n)] = placed.reshape(subsets, half_slices, width)
-        out_copy(n).start()
+            out_ref[:, there, cols(n)] = placed.reshape(subsets, half_slices, width)
 
     @pl.loop(0, chunks)
     def _(n):
@@ -382,7 +393,6 @@
 
         for j in range(PASSES - 1):
             hop_copy(j, n).wait_send()
-        out_copy(n).wait()
 
     for j in range(PASSES - 1):
         mid_copy(j).wait_send()
@@ -394,12 +404,12 @@
     chunk = rays // tiles
     hops = PASSES - 1
     dma = pltpu.SemaphoreType.DMA
-    hbm = pl.BlockSpec(memory_space=pl.ANY)
+    hbm = pl.BlockSpec(memory_space=pltpu.HBM)
     return pl.pallas_call(
         functools.partial(sweep_kernel, tiles),
         out_shape=jax.ShapeDtypeStruct((subsets, slices, vox), BF16),
         in_specs=[hbm] * 5,
-        out_specs=hbm,
+        out_specs=pl.BlockSpec(memory_space=pltpu.VMEM),
         scratch_shapes=[
             pltpu.VMEM(order.shape, jnp.int32),
             pltpu.VMEM(order.shape[::-1], jnp.int32),
@@ -422,7 +432,7 @@
             pltpu.VMEM((hops, slices, vox), BF16),
             pltpu.VMEM((slices, rays), F32),
             pltpu.VMEM((subsets, slices, vox), BF16),
-            dma((rays // (2 * chunk),)),
+            dma((rays // (GROUP * chunk),)),
             dma((4,)),
             dma((tiles,)),
             dma((PASSES, tiles)),
@@ -434,12 +444,11 @@
             dma((hops, chunks)),
             dma((9, chunks)),
             dma((9, chunks)),
-            dma((chunks,)),
         ],
         compiler_params=pltpu.CompilerParams(
-            collective_id=0, has_side_effects=True, vmem_limit_bytes=60 * 1024 * 1024
+            collective_id=0, has_side_effects=True, vmem_limit_bytes=VMEM_LIMIT
         ),
-    )(order, pattern, start, meas, system)
+    )(*(pltpu.with_memory_space_constraint(x, pltpu.HBM) for x in (order, pattern, start, meas, system)))
 
 
 def body(tiles, chunks, start_volume, measured, system_values, block_pattern, subset_order):

time: 145 us -> 139 us (0.959)
  Pallas kernels: 140 us -> 137 us
  local copies, waits for them, and re-layouts: 4.7 us -> 2.02 us
    pallas_call x1, Pallas kernels: 140 us -> 137 us  [sweep(): pl.pallas_call(functools.partial(sweep_kernel, tiles), out_shape=jax.Shap...]
    unnamed x1, local copies, waits for them, and re-layouts: 4.7 us -> 2.02 us
where the time goes in v4:
time: 139 us
  Pallas kernels  137 us (99%)
  local copies, waits for them, and re-layouts  2.02 us (1%)
    pallas_call x1, Pallas kernels, sweep(): pl.pallas_call(functools.partial(sweep_kernel, tiles), out_shape=jax.Shap...  137 us

profile of v4, /device:TPU:1, one launch (start us, length us, event | category | flops | bytes accessed | tf_op | source)
XLA Modules:
  0.0 139.0 jit_solution(204370986345236474)
XLA Ops:
  0.0 137.0 %shard_map.55 = bf16[8,64,4096]{2,1,0:T(8,128)(2,1)S(1)} custom-call(s32[8,64]{1,0:T(8,128)} %bitcast.1, s32[1,16,32]{2,1,0:T(8,128)} %pattern_hbm.1, bf16[8,64,4096]{2,1,0:T(8,128)(2,1)} %start_hbm.1, bf16[1,8,64,2048]{3,2,1,0:T(8,128)(2,1)} %meas_hbm.1, bf16[1,2048,4096]{2,1,0:T(8,128)(2,1)} %sys_hbm.1), custom_call_target="tpu_custom_call" | custom-call | tf_op jit(solution)/shard_map/pallas_call | solution.py:408
  137.0 2.0 %copy.7 = bf16[8,64,4096]{2,1,0:T(8,128)(2,1)} copy(bf16[8,64,4096]{2,1,0:T(8,128)(2,1)S(1)} %shard_map.55) | data formatting | bytes 8388608
